TPU v7x, 256 devices: a whole 4x4x8 slice. The times are simulated.
256 devices in a mesh: dp: 4 (over y), seq: 16 (over z, core), mp: 4 (over x).
Axes of the slice: x: 4, y: 4, z: 8, core: 2. Of those that a mesh axis runs over, the one named last changes fastest.
Arguments:
- q_self: bfloat16 [4, 1024, 4096], P('dp', 'seq', 'mp'), may hold values from -12 to 12
- k_self: bfloat16 [4, 1024, 4096], P('dp', 'seq', 'mp'), may hold values from -3 to 3
- v_self: bfloat16 [4, 1024, 4096], P('dp', 'seq', 'mp'), may hold values from -0.75 to 0.75
- out_grad_self: bfloat16 [4, 1024, 4096], P('dp', 'seq', 'mp'), may hold values from -6 to 6
- q_cross: bfloat16 [4, 1024, 4096], P('dp', 'seq', 'mp'), may hold values from -12 to 12
- k_cross: bfloat16 [4, 2048, 4096], P('dp', 'seq', 'mp'), may hold values from -3 to 3
- v_cross: bfloat16 [4, 2048, 4096], P('dp', 'seq', 'mp'), may hold values from -0.75 to 0.75
- out_grad_cross: bfloat16 [4, 1024, 4096], P('dp', 'seq', 'mp'), may hold values from -8 to 8
- dec_lengths: int32 [4, 16], P('dp'), may hold values from 1 to 640, as said below
- enc_lengths: int32 [4, 16], P('dp'), may hold values from 1 to 1280, as said below
- rel_bias: float32 [32, 64], P(None, 'mp'), may hold values from -4 to 4
Outputs:
- grad_q_self: bfloat16 [4, 1024, 4096], P('dp', 'seq', 'mp')
- grad_k_self: bfloat16 [4, 1024, 4096], P('dp', 'seq', 'mp')
- grad_v_self: bfloat16 [4, 1024, 4096], P('dp', 'seq', 'mp')
- grad_q_cross: bfloat16 [4, 1024, 4096], P('dp', 'seq', 'mp')
- grad_k_cross: bfloat16 [4, 2048, 4096], P('dp', 'seq', 'mp')
- grad_v_cross: bfloat16 [4, 2048, 4096], P('dp', 'seq', 'mp')
- bias_grad: float32 [32, 64], P(None, 'mp')
Inputs may be any that keep to these rules, and one draw needn't show every extreme that they name: `dec_lengths`: row p lists the decoder lengths of the 16 examples of pack p in order; they sum to 1024 and the largest is exactly 640. `enc_lengths`: row p lists the encoder lengths of the same 16 examples in the same order; they sum to 2048. The example with 640 decoder rows has exactly 1280 encoder rows; every other example has at least as many encoder rows as decoder rows and at most three times as many.
All inputs are finite; a program needn't handle non-finite values.
Results may differ from a plain program's by a relative error of at most 0.039.
Values may be sent and summed in bfloat16 or wider, within the bound.
A program may use at most 128 MiB of HBM per device.

v0:
```python
import math
import jax
import jax.numpy as jnp
from jax import lax
from jax.sharding import PartitionSpec as P

HEAD_DIM = 64
BUCKETS = 32
DISTANCE = 128


def bucket_of(distances):
    exact_count = BUCKETS // 2
    bucketed = jnp.full(distances.shape, exact_count, jnp.int32)
    for level_index in range(1, BUCKETS - exact_count):
        threshold = math.ceil(
            exact_count * (DISTANCE / exact_count) ** (level_index / (BUCKETS - exact_count))
        )
        bucketed = bucketed + (distances >= threshold).astype(jnp.int32)
    return jnp.where(distances < exact_count, distances, bucketed)


def example_ids(total_rows, lengths):
    segment_ends = jnp.cumsum(lengths)
    positions = jnp.arange(total_rows, dtype=jnp.int32)
    return jnp.sum((positions[:, None] >= segment_ends[None, :]).astype(jnp.int32), axis=1)


def distance_table(rel_bias, offset_base, table_span):
    distances = offset_base + jnp.arange(table_span, dtype=jnp.int32)
    buckets = bucket_of(jnp.maximum(distances, 0))
    one_hot = (buckets[None, :] == jnp.arange(rel_bias.shape[0], dtype=jnp.int32)[:, None]).astype(
        jnp.float32
    )
    bias_table = jnp.einsum("bh,bl->hl", rel_bias, one_hot, precision=lax.Precision.HIGHEST)
    return (one_hot, bias_table)


def spread(bias_table, row_count, col_count):
    full_span = row_count + col_count - 1
    leading = bias_table.shape[:-1]
    tiled_rows = jnp.broadcast_to(bias_table[..., None, :], leading + (row_count, full_span))
    flat_rows = tiled_rows.reshape(leading + (row_count * full_span,))
    flat_rows = jnp.pad(flat_rows, [(0, 0)] * len(leading) + [(0, row_count)])
    skewed = flat_rows.reshape(leading + (row_count, full_span + 1))[..., :col_count]
    return skewed[..., ::-1]


def collapse(matrix, row_count, col_count):
    full_span = row_count + col_count - 1
    leading = matrix.shape[:-2]
    flipped = matrix[..., ::-1]
    padded = jnp.pad(flipped, [(0, 0)] * len(leading) + [(0, 0), (0, row_count)])
    flat_rows = padded.reshape(leading + (row_count * (full_span + 1),))[
        ..., : row_count * full_span
    ]
    return jnp.sum(flat_rows.reshape(leading + (row_count, full_span)), axis=-2)


def shard_group(shard_count, row_count):
    group_size = 1
    while group_size < shard_count and (
        shard_count % group_size != 0 or group_size * row_count < 384
    ):
        group_size += 1
    return group_size


def query_side(
    queries,
    out_grads,
    all_keys,
    all_values,
    key_ids,
    query_ids,
    query_start,
    rel_bias,
    block_rows,
    causal,
):
    row_count, head_count, head_size = queries.shape
    block_count = all_keys.shape[0] // block_rows
    query_pos = query_start + jnp.arange(row_count, dtype=jnp.int32)
    block_ids = jnp.arange(block_count, dtype=jnp.int32)

    def scores_of(block_id):
        key_first = block_id * block_rows
        key_block = lax.dynamic_slice_in_dim(all_keys, key_first, block_rows, 0)
        key_block_ids = lax.dynamic_slice_in_dim(key_ids, key_first, block_rows, 0)
        scores = jnp.einsum("thd,uhd->htu", queries, key_block, preferred_element_type=jnp.float32)
        allowed = query_ids[:, None] == key_block_ids[None, :]
        one_hot = jnp.zeros((1, 1), jnp.float32)
        if causal:
            key_pos = key_first + jnp.arange(block_rows, dtype=jnp.int32)
            allowed = allowed & (query_pos[:, None] >= key_pos[None, :])
            one_hot, bias_table = distance_table(
                rel_bias, query_start - key_first - (block_rows - 1), row_count + block_rows - 1
            )
            scores = scores + spread(bias_table, row_count, block_rows)
        return (jnp.where(allowed[None], scores, -1e30), one_hot)

    def stat_step(running, block_id):
        row_high, total_sum = running
        scores, unused_hot = scores_of(block_id)
        new_high = jnp.maximum(row_high, jnp.max(scores, axis=2))
        total_sum = total_sum * jnp.exp(row_high - new_high) + jnp.sum(
            jnp.exp(scores - new_high[:, :, None]), axis=2
        )
        return ((new_high, total_sum), None)

    start_state = (
        jnp.full((head_count, row_count), -1e30, jnp.float32),
        jnp.zeros((head_count, row_count), jnp.float32),
    )
    (row_high, total_sum), unused_stats = lax.scan(stat_step, start_state, block_ids)

    def weights_of(scores):
        return jnp.exp(scores - row_high[:, :, None]) / total_sum[:, :, None]

    def out_step(summed, block_id):
        scores, unused_hot = scores_of(block_id)
        narrow_weights = weights_of(scores).astype(jnp.bfloat16)
        value_block = lax.dynamic_slice_in_dim(all_values, block_id * block_rows, block_rows, 0)
        return (
            summed
            + jnp.einsum(
                "htu,uhd->thd", narrow_weights, value_block, preferred_element_type=jnp.float32
            ),
            None,
        )

    summed, unused_outs = lax.scan(
        out_step, jnp.zeros((row_count, head_count, head_size), jnp.float32), block_ids
    )
    outputs = summed.astype(jnp.bfloat16)
    row_delta = jnp.einsum("thd,thd->ht", out_grads, outputs, preferred_element_type=jnp.float32)

    def grad_step(running, block_id):
        query_grad, bias_grad_sum = running
        scores, one_hot = scores_of(block_id)
        weights = weights_of(scores)
        narrow_weights = weights.astype(jnp.bfloat16)
        key_block = lax.dynamic_slice_in_dim(all_keys, block_id * block_rows, block_rows, 0)
        value_block = lax.dynamic_slice_in_dim(all_values, block_id * block_rows, block_rows, 0)
        weight_grads = jnp.einsum(
            "thd,uhd->htu", out_grads, value_block, preferred_element_type=jnp.float32
        )
        score_grads = weights * (weight_grads - row_delta[:, :, None])
        narrow_grads = score_grads.astype(jnp.bfloat16)
        query_grad = query_grad + jnp.einsum(
            "htu,uhd->thd", narrow_grads, key_block, preferred_element_type=jnp.float32
        )
        if causal:
            bias_grad_sum = bias_grad_sum + jnp.einsum(
                "hl,bl->bh",
                collapse(score_grads, row_count, block_rows),
                one_hot,
                precision=lax.Precision.HIGHEST,
            )
        key_term = jnp.einsum(
            "htu,thd->uhd", narrow_grads, queries, preferred_element_type=jnp.float32
        )
        value_term = jnp.einsum(
            "htu,thd->uhd", narrow_weights, out_grads, preferred_element_type=jnp.float32
        )
        grad_term = jnp.concatenate(
            [
                key_term.reshape(block_rows, head_count * head_size),
                value_term.reshape(block_rows, head_count * head_size),
            ],
            axis=1,
        ).astype(jnp.bfloat16)
        return ((query_grad, bias_grad_sum), grad_term)

    grad_state = (
        jnp.zeros((row_count, head_count, head_size), jnp.float32),
        jnp.zeros((rel_bias.shape[0], head_count), jnp.float32),
    )
    (query_grad, bias_grad_sum), grad_terms = lax.scan(grad_step, grad_state, block_ids)
    grad_terms = grad_terms.reshape(block_count * block_rows, 2 * head_count * head_size)
    query_grad = query_grad.astype(jnp.bfloat16).reshape(row_count, head_count * head_size)
    return (query_grad, grad_terms, bias_grad_sum, (row_high, total_sum, row_delta))


def on_device(
    q_self,
    k_self,
    v_self,
    out_grad_self,
    q_cross,
    k_cross,
    v_cross,
    out_grad_cross,
    dec_lengths,
    enc_lengths,
    rel_bias,
):
    seq_count = lax.axis_size("seq")
    seq_place = lax.axis_index("seq")
    dec_rows = q_self.shape[1]
    enc_rows = k_cross.shape[1]
    feature_count = q_self.shape[2]
    head_count = feature_count // HEAD_DIM
    dec_total = dec_rows * seq_count
    enc_total = enc_rows * seq_count
    dec_start = seq_place * dec_rows
    dec_ids = example_ids(dec_total, dec_lengths[0])
    enc_ids = example_ids(enc_total, enc_lengths[0])
    my_dec_ids = lax.dynamic_slice_in_dim(dec_ids, dec_start, dec_rows, 0)

    def split_heads(tensor):
        return tensor.reshape(tensor.shape[0] * tensor.shape[1], head_count, HEAD_DIM)

    gathered = (
        lax.all_gather(k_self, "seq", axis=1, tiled=True),
        lax.all_gather(v_self, "seq", axis=1, tiled=True),
        lax.all_gather(k_cross, "seq", axis=1, tiled=True),
        lax.all_gather(v_cross, "seq", axis=1, tiled=True),
    )
    self_group = shard_group(seq_count, dec_rows)
    cross_group = shard_group(seq_count, enc_rows)
    self_dq, self_terms, self_bias, self_stats = query_side(
        split_heads(q_self),
        split_heads(out_grad_self),
        split_heads(gathered[0]),
        split_heads(gathered[1]),
        dec_ids,
        my_dec_ids,
        dec_start,
        rel_bias,
        self_group * dec_rows,
        True,
    )
    cross_dq, cross_terms, unused_bias, cross_stats = query_side(
        split_heads(q_cross),
        split_heads(out_grad_cross),
        split_heads(gathered[2]),
        split_heads(gathered[3]),
        enc_ids,
        my_dec_ids,
        dec_start,
        rel_bias,
        cross_group * enc_rows,
        False,
    )
    self_sums = lax.psum_scatter(
        self_terms.astype(jnp.float32).astype(jnp.bfloat16), "seq", scatter_dimension=0, tiled=True
    ).astype(jnp.float32)
    cross_sums = lax.psum_scatter(
        cross_terms.astype(jnp.float32).astype(jnp.bfloat16), "seq", scatter_dimension=0, tiled=True
    ).astype(jnp.float32)
    self_key_grad = self_sums[:, :feature_count]
    self_value_grad = self_sums[:, feature_count:]
    cross_key_grad = cross_sums[:, :feature_count]
    cross_value_grad = cross_sums[:, feature_count:]
    bias_total = lax.psum(self_bias, ("dp", "seq"))
    bias_grad = bias_total * (1.0 / math.sqrt(lax.axis_size("dp") * dec_total))
    return (
        self_dq.reshape(1, dec_rows, feature_count),
        self_key_grad.reshape(1, dec_rows, feature_count).astype(jnp.bfloat16),
        self_value_grad.reshape(1, dec_rows, feature_count).astype(jnp.bfloat16),
        cross_dq.reshape(1, dec_rows, feature_count),
        cross_key_grad.reshape(1, enc_rows, feature_count).astype(jnp.bfloat16),
        cross_value_grad.reshape(1, enc_rows, feature_count).astype(jnp.bfloat16),
        bias_grad,
    )


def solution(mesh):
    return jax.shard_map(
        on_device,
        mesh=mesh,
        in_specs=(
            P("dp", "seq", "mp"),
            P("dp", "seq", "mp"),
            P("dp", "seq", "mp"),
            P("dp", "seq", "mp"),
            P("dp", "seq", "mp"),
            P("dp", "seq", "mp"),
            P("dp", "seq", "mp"),
            P("dp", "seq", "mp"),
            P("dp", None),
            P("dp", None),
            P(None, "mp"),
        ),
        out_specs=(
            P("dp", "seq", "mp"),
            P("dp", "seq", "mp"),
            P("dp", "seq", "mp"),
            P("dp", "seq", "mp"),
            P("dp", "seq", "mp"),
            P("dp", "seq", "mp"),
            P(None, "mp"),
        ),
        check_vma=False,
    )
```

profile of v0, /device:TPU:2, one launch (start us, length us, event | category | flops | bytes accessed | tf_op | source)
XLA Modules:
  0.0 455.4 jit_solution(5825784003897655049)
XLA Ops:
  17.9 34.6 %all-gather.5.cloned.1.call-done = bf16[1,1024,1024]{2,1,0:T(8,128)(2,1)} async-done(((bf16[1,64,1024]{2,1,0:T(8,128)(2,1)}), bf16[1,1024,1024]{2,1,0:T(8,128)(2,1)}) %all-gather.5.cloned.1.call-update) | async-done | bytes 2097168 | tf_op jit(solution)/shard_map/all_gather | solution.py:215
  52.6 3.9 copy.70
  56.5 31.9 %while.91 = (s32[]{:T(128)}, f32[16,64]{1,0:T(8,128)S(1)}, f32[16,64]{1,0:T(8,128)S(1)}, s32[64]{0:T(128)S(1)}, s32[2]{0:T(128)S(1)}, /*index=5*/s32[1024]{0:T(1...) while((s32[]{:T(128)}, f32[16,64]{1,0:T(8,128)S(1)}, ...), condition=%wide.region_5.6_spmd.clone.clone.clone, body=%wide.region_2.0_spmd.clone.clone.clone.sunk | while | flops 73413688 | bytes 34665884 | solution.py:115
  66.6 2.5 rev.40
  82.6 2.5 rev.40
  88.4 4.1 all-gather.7.cloned.1.call-done
  92.5 3.9 copy.74
  96.4 34.2 %while.92 = (s32[]{:T(128)}, f32[64,16,64]{0,2,1:T(8,128)}, s32[2]{0:T(128)S(1)}, bf16[1024,16,64]{0,2,1:T(8,128)(2,1)}, s32[64]{0:T(128)S(1)}, /*index=5*/s32[1...) while((s32[]{:T(128)}, f32[64,16,64]{0,2,1:T(8,128)}, ...), condition=%wide.region_7.8_spmd.clone.clone.clone, body=%wide.region_6.7_spmd.clone.clone.clone.sunk | while | flops 140648496 | bytes 34098144 | solution.py:132
  109.2 3.4 fusion.213
  126.3 3.4 fusion.213
  131.7 80.7 %while.93 = (s32[]{:T(128)}, f32[64,16,64]{0,2,1:T(8,128)}, f32[32,16]{0,1:T(8,128)S(1)}, bf16[2,512,2048]{2,1,0:T(8,128)(2,1)}, s32[2]{0:T(128)S(1)}, /*index=5...) while((s32[]{:T(128)}, f32[64,16,64]{0,2,1:T(8,128)}, ...), condition=%wide.region_10.11_spmd.clone.clone.clone, body=%wide.region_8.10_spmd.clone.clone.clone.sunk | while | flops 353446976 | bytes 101543680 | solution.py:179
  144.6 2.7 fusion.226
  154.3 2.5 rev.43
  164.8 3.7 reshape.726
  168.9 3.3 constant_dynamic-update-slice_fusion.5
  184.9 2.7 fusion.226
  205.1 3.7 reshape.726
  209.2 3.3 constant_dynamic-update-slice_fusion.5
  212.6 6.7 %copy.79 = bf16[1,2048,1024]{1,2,0:T(8,128)(2,1)} copy(bf16[1,2048,1024]{2,1,0:T(8,128)(2,1)} %all-gather.9.cloned.1.call-done) | data formatting | bytes 8388608 | tf_op jit(solution)/shard_map/all_gather | solution.py:217
  219.4 15.2 %while.88 = (s32[]{:T(128)}, f32[16,64]{1,0:T(8,128)S(1)}, f32[16,64]{1,0:T(8,128)S(1)}, s32[64]{0:T(128)S(1)}, s32[4]{0:T(128)S(1)}, /*index=5*/s32[2048]{0:T(1...) while((s32[]{:T(128)}, f32[16,64]{1,0:T(8,128)S(1)}, ...), condition=%wide.region_17.18_spmd.clone, body=%wide.region_14.17_spmd.clone.sunk | while | flops 69768200 | bytes 5532106 | solution.py:115
  234.6 6.6 %copy.83 = bf16[1,2048,1024]{1,2,0:T(8,128)(2,1)} copy(bf16[1,2048,1024]{2,1,0:T(8,128)(2,1)} %all-gather.11.cloned.1.call-done) | data formatting | bytes 8388608 | tf_op jit(solution)/shard_map/all_gather | solution.py:218
  241.3 16.1 %while.89 = (s32[]{:T(128)}, f32[64,16,64]{0,2,1:T(8,128)S(1)}, s32[4]{0:T(128)S(1)}, bf16[2048,16,64]{0,2,1:T(8,128)(2,1)}, s32[64]{0:T(128)S(1)}, /*index=5*/s...) while((s32[]{:T(128)}, f32[64,16,64]{0,2,1:T(8,128)S(1)}, ...), condition=%wide.region_19.20_spmd.clone, body=%wide.region_18.19_spmd.clone.sunk | while | flops 136478720 | bytes 2834388 | solution.py:132
  242.7 2.6 fusion.191
  246.7 2.6 fusion.191
  250.8 2.5 fusion.191
  254.8 2.6 fusion.191
  257.5 54.1 %while.90 = (s32[]{:T(128)}, f32[64,16,64]{0,2,1:T(8,128)S(1)}, bf16[4,512,2048]{2,1,0:T(8,128)(2,1)}, s32[4]{0:T(128)S(1)}, bf16[2048,16,64]{0,2,1:T(8,128)(2,1...) while((s32[]{:T(128)}, f32[64,16,64]{0,2,1:T(8,128)S(1)}, ...), condition=%wide.region_21.22_spmd.clone, body=%wide.region_20.21_spmd.clone.sunk | while | flops 344621056 | bytes 28396028 | solution.py:179
  266.6 2.9 copy.116
  280.2 2.9 copy.116
  293.6 2.9 copy.116
  307.1 2.9 copy.116
  313.4 130.1 %psum.7 = f32[32,16]{0,1:T(8,128)S(1)} all-reduce(f32[32,16]{0,1:T(8,128)S(1)} %get-tuple-element.693), channel_id=1, replica_groups=mesh['dp'=4,'seq'=16,'mp'=4] {'dp','seq'}, use_global_device_ids=true, to_apply=%region_23.24 | all-reduce | flops 512 | bytes 4096 | tf_op jit(solution)/shard_map/psum | solution.py:256
  (310 shorter events, 181.8 us)
Async XLA Ops:
  7.2 9.6 %copy-start.19 = (bf16[1,64,1024]{2,1,0:T(8,128)(2,1)S(1)}, bf16[1,64,1024]{2,1,0:T(8,128)(2,1)}, u32[]{:S(2)}) copy-start(bf16[1,64,1024]{2,1,0:T(8,128)(2,1)} %param.27) | copy-start | bytes 393220
  7.2 45.4 %all-gather.5.cloned.1.call-start = ((), (), s32[]{:S(2)}) async-start(), calls=%async_computation.2 | async-start | bytes 2228224 | tf_op jit(solution)/shard_map/all_gather | solution.py:215
  7.9 84.5 %all-gather.7.cloned.1.call-start = ((), (), s32[]{:S(2)}) async-start(), calls=%async_computation.3 | async-start | bytes 2228224 | tf_op jit(solution)/shard_map/all_gather | solution.py:216
  8.7 203.9 %all-gather.9.cloned.1.call-start = ((), (), s32[]{:S(2)}) async-start(), calls=%async_computation.5 | async-start | bytes 4456448 | tf_op jit(solution)/shard_map/all_gather | solution.py:217
  9.4 225.2 %all-gather.11.cloned.1.call-start = ((), (), s32[]{:S(2)}) async-start(), calls=%async_computation.6 | async-start | bytes 4456448 | tf_op jit(solution)/shard_map/all_gather | solution.py:218
  10.0 435.0 %reduce-scatter.3.cloned.1.call-start = ((), (), s32[]{:S(2)}) async-start(), calls=%async_computation.4 | async-start | bytes 4456448 | tf_op jit(solution)/shard_map/reduce_scatter | solution.py:246
  17.0 39.5 %copy-start.7 = (bf16[1,64,1024]{1,2,0:T(8,128)(2,1)}, bf16[1,64,1024]{1,2,0:T(8,128)(2,1)S(1)}, u32[]{:S(2)}) copy-start(bf16[1,64,1024]{1,2,0:T(8,128)(2,1)S(1)} %copy.81) | copy-start | bytes 393220
  17.9 38.6 %copy-start.12 = (f32[32,16]{0,1:T(8,128)S(1)}, f32[32,16]{0,1:T(8,128)}, u32[]{:S(2)}) copy-start(f32[32,16]{0,1:T(8,128)} %param.33) | copy-start | bytes 6148
  81.0 1.6 slice-start
  105.1 1.6 slice-start.1
  106.7 2.5 copy-start.15
  122.2 1.6 slice-start.1
  123.8 2.5 copy-start.15
  131.9 12.7 %copy-start.9 = (bf16[64,16,64]{0,2,1:T(8,128)(2,1)}, bf16[64,16,64]{0,2,1:T(8,128)(2,1)S(1)}, u32[]{:S(2)}) copy-start(bf16[64,16,64]{0,2,1:T(8,128)(2,1)S(1)} %get-tuple-element.1967) | copy-start | bytes 393220 | tf_op jit(solution)/shard_map/while
  140.5 1.6 slice-start.2
  147.3 1.6 copy-start.2
  148.8 1.6 copy-start
  148.9 1.7 copy-start.3
  168.9 3.3 copy-start.10
  172.3 12.7 %copy-start.9 = (bf16[64,16,64]{0,2,1:T(8,128)(2,1)}, bf16[64,16,64]{0,2,1:T(8,128)(2,1)S(1)}, u32[]{:S(2)}) copy-start(bf16[64,16,64]{0,2,1:T(8,128)(2,1)S(1)} %get-tuple-element.1967) | copy-start | bytes 393220 | tf_op jit(solution)/shard_map/while
  187.6 1.6 copy-start.2
  189.2 1.7 copy-start.3
  209.2 3.3 copy-start.10
  212.5 6.9 %copy-start.11 = (bf16[64,16,64]{2,0,1:T(8,128)(2,1)S(1)}, bf16[64,16,64]{2,0,1:T(8,128)(2,1)}, u32[]{:S(2)}) copy-start(bf16[64,16,64]{2,0,1:T(8,128)(2,1)} %copy.82) | copy-start | bytes 393220
  212.5 6.8 %copy-start.13 = (f32[16,64]{1,0:T(8,128)S(1)}, f32[16,64]{1,0:T(8,128)}, u32[]{:S(2)}) copy-start(f32[16,64]{1,0:T(8,128)} %custom-call.5) | copy-start | bytes 12292
  212.5 6.8 %copy-start.17 = (f32[16,64]{1,0:T(8,128)S(1)}, f32[16,64]{1,0:T(8,128)}, u32[]{:S(2)}) copy-start(f32[16,64]{1,0:T(8,128)} %custom-call.6) | copy-start | bytes 12292
  212.5 6.8 %copy-start.18 = (s32[2048]{0:T(1024)S(1)}, s32[2048]{0:T(1024)}, u32[]{:S(2)}) copy-start(s32[2048]{0:T(1024)} %convert_reduce_fusion) | copy-start | bytes 24580
  212.5 234.2 %reduce-scatter.5.cloned.1.call-start = ((), (), s32[]{:S(2)}) async-start(), calls=%async_computation.7 | async-start | bytes 8912896 | tf_op jit(solution)/shard_map/reduce_scatter | solution.py:249
  234.6 6.7 %copy-start.14 = (f32[64,16,64]{0,2,1:T(8,128)S(1)}, f32[64,16,64]{0,2,1:T(8,128)}, u32[]{:S(2)}) copy-start(f32[64,16,64]{0,2,1:T(8,128)} %custom-call.7) | copy-start | bytes 786436
  241.3 16.1 %copy-start.1 = (bf16[1,64,1024]{1,2,0:T(8,128)(2,1)S(1)}, bf16[1,64,1024]{1,2,0:T(8,128)(2,1)}, u32[]{:S(2)}) copy-start(bf16[1,64,1024]{1,2,0:T(8,128)(2,1)} %copy.84) | copy-start | bytes 393220
  241.3 16.2 %copy-start.6 = (f32[64,16,64]{0,2,1:T(8,128)S(1)}, f32[64,16,64]{0,2,1:T(8,128)}, u32[]{:S(2)}) copy-start(f32[64,16,64]{0,2,1:T(8,128)} %custom-call.8) | copy-start | bytes 786436
  241.3 16.2 %copy-start.8 = (bf16[1,64,1024]{1,2,0:T(8,128)(2,1)S(1)}, bf16[1,64,1024]{1,2,0:T(8,128)(2,1)}, u32[]{:S(2)}) copy-start(bf16[1,64,1024]{1,2,0:T(8,128)(2,1)} %copy-done.7) | copy-start | bytes 393220
  (8 other events, 9.2 us)
Sparse Core Ops, SparseCore 0:
  9.8 42.6 all-gather.4
  54.4 38.0 all-gather.6
  94.3 40.5 all-gather.8
  136.5 40.8 all-gather.10
  212.6 61.6 reduce-scatter.2
  311.7 69.7 reduce-scatter.4
where the time goes:
time: 458 us; the launch traced here: 455 us
  local copies, waits for them, and re-layouts  170 us (37%)
  blocking collectives  130 us (28%)
  matrix products  67.9 us (15%)
  waiting for transfers between devices  41.4 us (9%)
  other arithmetic  17.8 us (4%)
  between operations  14.5 us (3%)
  loops' own time  13.3 us (3%)
    psum x1, blocking collectives, on_device(): bias_total = lax.psum(self_bias, ('dp', 'seq'))  130 us
    all_gather x1, waiting for transfers between devices, on_device(): lax.all_gather(k_self, 'seq', axis=1, tiled=True)  34.6 us
    dynamic_update_slice x12, local copies, waits for them, and re-layouts, query_side(): lax.scan(grad_step, grad_state, block_ids)  29.1 us
    dot_general x12, matrix products, scores_of(): jnp.einsum('thd,uhd->htu', queries, key_block, preferred_element_type=jnp...  24.8 us
    dot_general x6, matrix products, out_step(): jnp.einsum('htu,uhd->thd', narrow_weights, value_block, preferred_element...  17.1 us
    rev x6, local copies, waits for them, and re-layouts, spread(): return skewed[..., ::-1]  15.1 us
    reshape x6, local copies, waits for them, and re-layouts, spread(): flat_rows = tiled_rows.reshape(leading + (row_count * full_span,))  14.9 us
    reshape x6, local copies, waits for them, and re-layouts, spread(): flat_rows.reshape(leading + (row_count, full_span + 1))[..., :col_count]  14.6 us
  transfers between devices with their start and end apart: 6, of which 2 were waited for; matrix products, arithmetic and copies ran while one was open for 52% of the time, Pallas kernels for 0%

commit v1 on v0

--- a/solution.py
+++ b/solution.py
@@ -253,7 +253,8 @@
     self_value_grad = self_sums[:, feature_count:]
     cross_key_grad = cross_sums[:, :feature_count]
     cross_value_grad = cross_sums[:, feature_count:]
-    bias_total = lax.psum(self_bias, ("dp", "seq"))
+    one_axis = lax.psum(self_bias, "seq")
+    bias_total = lax.psum(one_axis, "dp")
     bias_grad = bias_total * (1.0 / math.sqrt(lax.axis_size("dp") * dec_total))
     return (
         self_dq.reshape(1, dec_rows, feature_count),

time: 458 us -> 393 us (0.86)
  blocking collectives: 130 us -> 36.4 us
  waiting for transfers between devices: 41.4 us -> 69.6 us
    psum x1 -> x2, blocking collectives: 130 us -> 36.4 us  [the longest x1 25.8 us: on_device(): one_axis = lax.psum(self_bias, 'seq')]
    reduce_scatter x1, waiting for transfers between devices: 0.01 us -> 28 us  [on_device(): lax.psum_scatter(cross_terms.astype(jnp.float32).astype(jnp.bfloat16), 's...]
  transfers between devices with their start and end apart: 6 -> 6, of which waited for: 2 -> 3; matrix products, arithmetic and copies ran while one was open for 52% -> 60% of each run, Pallas kernels for 0% -> 0%
where the time goes in v1:
time: 393 us; the launch traced here: 390 us
  local copies, waits for them, and re-layouts  170 us (43%)
  waiting for transfers between devices  69.6 us (18%)
  matrix products  67.9 us (17%)
  blocking collectives  36.4 us (9%)
  other arithmetic  17.9 us (5%)
  between operations  14.5 us (4%)
  loops' own time  13 us (3%)
    all_gather x1, waiting for transfers between devices, on_device(): lax.all_gather(k_self, 'seq', axis=1, tiled=True)  34.6 us
    dynamic_update_slice x12, local copies, waits for them, and re-layouts, query_side(): lax.scan(grad_step, grad_state, block_ids)  29.1 us
    reduce_scatter x1, waiting for transfers between devices, on_device(): lax.psum_scatter(cross_terms.astype(jnp.float32).astype(jnp.bfloat16), 's...  28 us
    psum x1, blocking collectives, on_device(): one_axis = lax.psum(self_bias, 'seq')  25.8 us
    dot_general x12, matrix products, scores_of(): jnp.einsum('thd,uhd->htu', queries, key_block, preferred_element_type=jnp...  24.8 us
    dot_general x6, matrix products, out_step(): jnp.einsum('htu,uhd->thd', narrow_weights, value_block, preferred_element...  17.1 us
    rev x6, local copies, waits for them, and re-layouts, spread(): return skewed[..., ::-1]  15 us
    reshape x6, local copies, waits for them, and re-layouts, spread(): flat_rows = tiled_rows.reshape(leading + (row_count * full_span,))  14.9 us
  transfers between devices with their start and end apart: 6, of which 3 were waited for; matrix products, arithmetic and copies ran while one was open for 60% of the time, Pallas kernels for 0%

profile of v1, /device:TPU:2, one launch (start us, length us, event | category | flops | bytes accessed | tf_op | source)
XLA Modules:
  0.0 389.7 jit_solution(881093316746928909)
XLA Ops:
  17.9 34.6 %all-gather.5.cloned.1.call-done = bf16[1,1024,1024]{2,1,0:T(8,128)(2,1)} async-done(((bf16[1,64,1024]{2,1,0:T(8,128)(2,1)}), bf16[1,1024,1024]{2,1,0:T(8,128)(2,1)}) %all-gather.5.cloned.1.call-update) | async-done | bytes 2097168 | tf_op jit(solution)/shard_map/all_gather | solution.py:215
  52.6 3.9 %copy.70 = bf16[1,1024,1024]{1,2,0:T(8,128)(2,1)} copy(bf16[1,1024,1024]{2,1,0:T(8,128)(2,1)} %all-gather.5.cloned.1.call-done) | data formatting | bytes 4194304 | tf_op jit(solution)/shard_map/all_gather | solution.py:215
  56.5 31.7 %while.91 = (s32[]{:T(128)}, f32[16,64]{1,0:T(8,128)S(1)}, f32[16,64]{1,0:T(8,128)S(1)}, s32[64]{0:T(128)S(1)}, s32[2]{0:T(128)S(1)}, /*index=5*/s32[1024]{0:T(1...) while((s32[]{:T(128)}, f32[16,64]{1,0:T(8,128)S(1)}, ...), condition=%wide.region_5.6_spmd.clone.clone.clone, body=%wide.region_2.0_spmd.clone.clone.clone.sunk | while | flops 73413688 | bytes 34665884 | solution.py:115
  88.2 4.3 %all-gather.7.cloned.1.call-done = bf16[1,1024,1024]{2,1,0:T(8,128)(2,1)} async-done(((bf16[1,64,1024]{2,1,0:T(8,128)(2,1)}), bf16[1,1024,1024]{2,1,0:T(8,128)(2,1)}) %all-gather.7.cloned.1.call-update) | async-done | bytes 2097168 | tf_op jit(solution)/shard_map/all_gather | solution.py:216
  92.5 3.9 %copy.74 = bf16[1,1024,1024]{1,2,0:T(8,128)(2,1)} copy(bf16[1,1024,1024]{2,1,0:T(8,128)(2,1)} %all-gather.7.cloned.1.call-done) | data formatting | bytes 4194304 | tf_op jit(solution)/shard_map/all_gather | solution.py:216
  96.4 33.9 %while.92 = (s32[]{:T(128)}, f32[64,16,64]{0,2,1:T(8,128)}, s32[2]{0:T(128)S(1)}, bf16[1024,16,64]{0,2,1:T(8,128)(2,1)}, s32[64]{0:T(128)S(1)}, /*index=5*/s32[1...) while((s32[]{:T(128)}, f32[64,16,64]{0,2,1:T(8,128)}, ...), condition=%wide.region_7.8_spmd.clone.clone.clone, body=%wide.region_6.7_spmd.clone.clone.clone.sunk | while | flops 140648496 | bytes 34098144 | solution.py:132
  109.1 3.4 fusion.213
  126.1 3.4 fusion.213
  131.5 81.0 %while.93 = (s32[]{:T(128)}, f32[64,16,64]{0,2,1:T(8,128)}, f32[32,16]{0,1:T(8,128)S(1)}, bf16[2,512,2048]{2,1,0:T(8,128)(2,1)}, s32[2]{0:T(128)S(1)}, /*index=5...) while((s32[]{:T(128)}, f32[64,16,64]{0,2,1:T(8,128)}, ...), condition=%wide.region_10.11_spmd.clone.clone.clone, body=%wide.region_8.10_spmd.clone.clone.clone.sunk | while | flops 353446976 | bytes 101543680 | solution.py:179
  144.4 2.7 fusion.226
  164.7 3.8 reshape.726
  168.9 3.3 constant_dynamic-update-slice_fusion.5
  184.9 2.7 fusion.226
  194.5 2.5 rev.43
  205.1 3.7 reshape.726
  209.2 3.3 constant_dynamic-update-slice_fusion.5
  212.6 6.7 %copy.79 = bf16[1,2048,1024]{1,2,0:T(8,128)(2,1)} copy(bf16[1,2048,1024]{2,1,0:T(8,128)(2,1)} %all-gather.9.cloned.1.call-done) | data formatting | bytes 8388608 | tf_op jit(solution)/shard_map/all_gather | solution.py:217
  219.4 15.2 %while.88 = (s32[]{:T(128)}, f32[16,64]{1,0:T(8,128)S(1)}, f32[16,64]{1,0:T(8,128)S(1)}, s32[64]{0:T(128)S(1)}, s32[4]{0:T(128)S(1)}, /*index=5*/s32[2048]{0:T(1...) while((s32[]{:T(128)}, f32[16,64]{1,0:T(8,128)S(1)}, ...), condition=%wide.region_17.18_spmd.clone, body=%wide.region_14.17_spmd.clone.sunk | while | flops 69768200 | bytes 5532106 | solution.py:115
  234.7 6.6 %copy.83 = bf16[1,2048,1024]{1,2,0:T(8,128)(2,1)} copy(bf16[1,2048,1024]{2,1,0:T(8,128)(2,1)} %all-gather.11.cloned.1.call-done) | data formatting | bytes 8388608 | tf_op jit(solution)/shard_map/all_gather | solution.py:218
  241.3 16.1 %while.89 = (s32[]{:T(128)}, f32[64,16,64]{0,2,1:T(8,128)S(1)}, s32[4]{0:T(128)S(1)}, bf16[2048,16,64]{0,2,1:T(8,128)(2,1)}, s32[64]{0:T(128)S(1)}, /*index=5*/s...) while((s32[]{:T(128)}, f32[64,16,64]{0,2,1:T(8,128)S(1)}, ...), condition=%wide.region_19.20_spmd.clone, body=%wide.region_18.19_spmd.clone.sunk | while | flops 136478720 | bytes 2834388 | solution.py:132
  242.7 2.6 fusion.191
  246.7 2.6 fusion.191
  250.8 2.5 fusion.191
  254.8 2.6 fusion.191
  257.5 54.1 %while.90 = (s32[]{:T(128)}, f32[64,16,64]{0,2,1:T(8,128)S(1)}, bf16[4,512,2048]{2,1,0:T(8,128)(2,1)}, s32[4]{0:T(128)S(1)}, bf16[2048,16,64]{0,2,1:T(8,128)(2,1...) while((s32[]{:T(128)}, f32[64,16,64]{0,2,1:T(8,128)S(1)}, ...), condition=%wide.region_21.22_spmd.clone, body=%wide.region_20.21_spmd.clone.sunk | while | flops 344621056 | bytes 28396028 | solution.py:179
  266.7 3.0 copy.116
  280.2 2.9 copy.116
  293.7 2.9 copy.116
  307.2 2.9 copy.116
  313.5 25.8 %psum.14 = f32[32,16]{0,1:T(8,128)S(1)} all-reduce(f32[32,16]{0,1:T(8,128)S(1)} %get-tuple-element.693), channel_id=1, replica_groups=mesh['dp'=4,'seq'=16,'mp'=4] {'seq'}, use_global_device_ids=true, to_apply=%region_23.24 | all-reduce | flops 512 | bytes 4096 | tf_op jit(solution)/shard_map/psum | solution.py:256
  339.3 10.6 %psum.15 = f32[32,16]{0,1:T(8,128)S(1)} all-reduce(f32[32,16]{0,1:T(8,128)S(1)} %psum.14), channel_id=1, replica_groups=mesh['dp'=4,'seq'=16,'mp'=4] {'dp'}, use_global_device_ids=true, to_apply=%region_24.25 | all-reduce | flops 512 | bytes 4096 | tf_op jit(solution)/shard_map/psum | solution.py:257
  353.0 28.0 %reduce-scatter.5.cloned.1.call-done = bf16[128,2048]{1,0:T(8,128)(2,1)} async-done(((bf16[2048,2048]{1,0:T(8,128)(2,1)}), bf16[128,2048]{1,0:T(8,128)(2,1)}) %reduce-scatter.5.cloned.1.call-update) | async-done | bytes 524304 | tf_op jit(solution)/shard_map/reduce_scatter | solution.py:249
  (311 shorter events, 186.9 us)
Async XLA Ops:
  7.2 9.6 %copy-start.19 = (bf16[1,64,1024]{2,1,0:T(8,128)(2,1)S(1)}, bf16[1,64,1024]{2,1,0:T(8,128)(2,1)}, u32[]{:S(2)}) copy-start(bf16[1,64,1024]{2,1,0:T(8,128)(2,1)} %param.27) | copy-start | bytes 393220
  7.2 45.4 %all-gather.5.cloned.1.call-start = ((), (), s32[]{:S(2)}) async-start(), calls=%async_computation.2 | async-start | bytes 2228224 | tf_op jit(solution)/shard_map/all_gather | solution.py:215
  7.9 84.5 %all-gather.7.cloned.1.call-start = ((), (), s32[]{:S(2)}) async-start(), calls=%async_computation.3 | async-start | bytes 2228224 | tf_op jit(solution)/shard_map/all_gather | solution.py:216
  8.7 203.9 %all-gather.9.cloned.1.call-start = ((), (), s32[]{:S(2)}) async-start(), calls=%async_computation.5 | async-start | bytes 4456448 | tf_op jit(solution)/shard_map/all_gather | solution.py:217
  9.4 225.3 %all-gather.11.cloned.1.call-start = ((), (), s32[]{:S(2)}) async-start(), calls=%async_computation.6 | async-start | bytes 4456448 | tf_op jit(solution)/shard_map/all_gather | solution.py:218
  10.0 341.4 %reduce-scatter.3.cloned.1.call-start = ((), (), s32[]{:S(2)}) async-start(), calls=%async_computation.4 | async-start | bytes 4456448 | tf_op jit(solution)/shard_map/reduce_scatter | solution.py:246
  17.0 39.5 %copy-start.7 = (bf16[1,64,1024]{1,2,0:T(8,128)(2,1)}, bf16[1,64,1024]{1,2,0:T(8,128)(2,1)S(1)}, u32[]{:S(2)}) copy-start(bf16[1,64,1024]{1,2,0:T(8,128)(2,1)S(1)} %copy.81) | copy-start | bytes 393220
  17.9 38.6 %copy-start.12 = (f32[32,16]{0,1:T(8,128)S(1)}, f32[32,16]{0,1:T(8,128)}, u32[]{:S(2)}) copy-start(f32[32,16]{0,1:T(8,128)} %param.33) | copy-start | bytes 6148
  64.9 1.6 slice-start
  106.6 2.5 copy-start.15
  122.0 1.6 slice-start.1
  123.6 2.5 copy-start.15
  131.7 12.7 %copy-start.9 = (bf16[64,16,64]{0,2,1:T(8,128)(2,1)}, bf16[64,16,64]{0,2,1:T(8,128)(2,1)S(1)}, u32[]{:S(2)}) copy-start(bf16[64,16,64]{0,2,1:T(8,128)(2,1)S(1)} %get-tuple-element.1967) | copy-start | bytes 393220 | tf_op jit(solution)/shard_map/while
  140.3 1.6 slice-start.2
  147.0 1.6 copy-start.2
  148.6 1.7 copy-start.3
  168.9 3.3 copy-start.10
  172.2 12.7 %copy-start.9 = (bf16[64,16,64]{0,2,1:T(8,128)(2,1)}, bf16[64,16,64]{0,2,1:T(8,128)(2,1)S(1)}, u32[]{:S(2)}) copy-start(bf16[64,16,64]{0,2,1:T(8,128)(2,1)S(1)} %get-tuple-element.1967) | copy-start | bytes 393220 | tf_op jit(solution)/shard_map/while
  180.8 1.6 slice-start.2
  187.5 1.6 copy-start.2
  189.1 1.6 copy-start
  189.1 1.7 copy-start.3
  209.2 3.3 copy-start.10
  212.5 6.9 %copy-start.11 = (bf16[64,16,64]{2,0,1:T(8,128)(2,1)S(1)}, bf16[64,16,64]{2,0,1:T(8,128)(2,1)}, u32[]{:S(2)}) copy-start(bf16[64,16,64]{2,0,1:T(8,128)(2,1)} %copy.82) | copy-start | bytes 393220
  212.5 6.9 %copy-start.13 = (f32[16,64]{1,0:T(8,128)S(1)}, f32[16,64]{1,0:T(8,128)}, u32[]{:S(2)}) copy-start(f32[16,64]{1,0:T(8,128)} %custom-call.5) | copy-start | bytes 12292
  212.5 6.9 %copy-start.17 = (f32[16,64]{1,0:T(8,128)S(1)}, f32[16,64]{1,0:T(8,128)}, u32[]{:S(2)}) copy-start(f32[16,64]{1,0:T(8,128)} %custom-call.6) | copy-start | bytes 12292
  212.5 6.9 %copy-start.18 = (s32[2048]{0:T(1024)S(1)}, s32[2048]{0:T(1024)}, u32[]{:S(2)}) copy-start(s32[2048]{0:T(1024)} %convert_reduce_fusion) | copy-start | bytes 24580
  212.5 168.5 %reduce-scatter.5.cloned.1.call-start = ((), (), s32[]{:S(2)}) async-start(), calls=%async_computation.7 | async-start | bytes 8912896 | tf_op jit(solution)/shard_map/reduce_scatter | solution.py:249
  234.6 6.6 %copy-start.14 = (f32[64,16,64]{0,2,1:T(8,128)S(1)}, f32[64,16,64]{0,2,1:T(8,128)}, u32[]{:S(2)}) copy-start(f32[64,16,64]{0,2,1:T(8,128)} %custom-call.7) | copy-start | bytes 786436
  241.3 16.1 %copy-start.1 = (bf16[1,64,1024]{1,2,0:T(8,128)(2,1)S(1)}, bf16[1,64,1024]{1,2,0:T(8,128)(2,1)}, u32[]{:S(2)}) copy-start(bf16[1,64,1024]{1,2,0:T(8,128)(2,1)} %copy.84) | copy-start | bytes 393220
  241.3 16.2 %copy-start.6 = (f32[64,16,64]{0,2,1:T(8,128)S(1)}, f32[64,16,64]{0,2,1:T(8,128)}, u32[]{:S(2)}) copy-start(f32[64,16,64]{0,2,1:T(8,128)} %custom-call.8) | copy-start | bytes 786436
  241.3 16.2 %copy-start.8 = (bf16[1,64,1024]{1,2,0:T(8,128)(2,1)S(1)}, bf16[1,64,1024]{1,2,0:T(8,128)(2,1)}, u32[]{:S(2)}) copy-start(bf16[1,64,1024]{1,2,0:T(8,128)(2,1)} %copy-done.7) | copy-start | bytes 393220
  (8 other events, 9.2 us)
Sparse Core Ops, SparseCore 0:
  9.8 42.6 all-gather.4
  54.4 38.0 all-gather.6
  94.3 40.5 all-gather.8
  136.6 40.8 all-gather.10
  212.6 61.5 reduce-scatter.2
  311.7 69.2 reduce-scatter.4
